TPU v7x, 128 devices: a whole 4x4x4 slice. The times are simulated.
128 devices in a mesh: polar: 16 (over y_hi, z, core), azimuth: 8 (over y_lo, x).
Axes of the slice: x: 4, y: 4 (y_hi: 2, y_lo: 2; y = y_hi * 2 + y_lo), z: 4, core: 2. Of those that a mesh axis runs over, the one named last changes fastest.
Arguments:
- signal: bfloat16 [1024, 768, 256], P('polar', 'azimuth'), may hold values from -6 to 6
- cotangent: bfloat16 [1024, 768, 256], P('polar', 'azimuth'), may hold values from -6 to 6
- mixing: bfloat16 [2, 256, 256], replicated, may hold values from -0.25 to 0.25
- coupling: bfloat16 [16, 6, 64, 64], replicated, may hold values from -0.75 to 0.75
- filters: float32 [16, 6, 2, 384], P(None, None, None, 'azimuth'), may hold values from -4 to 4
- band_counts: int32 [16], replicated, may hold values from 2 to 6, as said below
- band_offsets: int32 [16, 6], replicated, may hold values from -1 to 1, as said below
- band_basis: int32 [16, 6], replicated, may hold values from 0 to 1
Outputs:
- output: bfloat16 [1024, 768, 256], P('polar', 'azimuth')
- signal_grad: bfloat16 [1024, 768, 256], P('polar', 'azimuth')
Inputs may be any that keep to these rules, and one draw needn't show every extreme that they name: `band_counts`: blocks 1 and 14 use all 6 slots; the two end blocks use at most 4. `band_offsets`: for every block b, the first band_counts[b] slots name distinct pairs of offset and basis, and b plus the offset lies in 0 to 15; later slots are unused.
All inputs are finite; a program needn't handle non-finite values.
Results may differ from a plain program's by a relative error of at most 0.0075.
Values may be sent and summed in bfloat16 or wider, within the bound.
No kernel may reach another device: no remote copies, remote signals or barrier semaphores. Data moves between devices by JAX's collectives and lax.ppermute only.
A program may use at most 192 MiB of HBM per device.

v0:
```python
import math

import jax
import jax.numpy as jnp
from jax import lax
from jax.sharding import PartitionSpec as P

NLON = 768
M = 384
K = 2
BLOCK = 64


def extended(cells, sides, width):
    for axis, dim in sides:
        count = lax.axis_size(axis)
        ends = count - 1
        head = lax.slice_in_dim(cells, 0, width, axis=dim)
        tail = lax.slice_in_dim(cells, cells.shape[dim] - width, cells.shape[dim], axis=dim)
        cells = jnp.concatenate(
            [
                lax.ppermute(tail, axis, [(i, (i + 1) % count) for i in range(ends)]),
                cells,
                lax.ppermute(head, axis, [((i + 1) % count, i) for i in range(ends)]),
            ],
            axis=dim,
        )
    return cells


def spectral_tables():
    longitude = jnp.arange(NLON, dtype=jnp.int32)
    wavenumber = jnp.arange(M, dtype=jnp.int32)
    product_mod = longitude[:, None] * wavenumber[None, :] % NLON
    phase_angle = product_mod.astype(jnp.float32) * (2.0 * math.pi / NLON)
    cosine = jnp.cos(phase_angle)
    sine_part = jnp.sin(phase_angle)
    forward = jnp.stack([cosine, -sine_part], axis=1).astype(jnp.bfloat16)
    weight = jnp.where(wavenumber == 0, 1.0, 2.0).astype(jnp.float32) / NLON
    inverse = jnp.transpose(
        jnp.stack([cosine, -sine_part], axis=0) * weight[None, None, :], (2, 0, 1)
    ).astype(jnp.bfloat16)
    return (forward, inverse)


def apply_filter(filt, coupled, conjugate):
    real_part = filt[0][:, None, None]
    imag_part = filt[1][:, None, None]
    if conjugate:
        imag_part = -imag_part
    leading = real_part * coupled[:, 0] - imag_part * coupled[:, 1]
    trailing = real_part * coupled[:, 1] + imag_part * coupled[:, 0]
    return jnp.stack([leading, trailing], axis=1)


def rows_of(rims, member, start_row):
    mode_local = rims.shape[0]
    piece = lax.dynamic_slice(
        rims, (0, member, 0, start_row, 0), (mode_local, 1, 2, BLOCK, rims.shape[4])
    )
    return piece[:, 0]


def per_device(signal, cotangent, mixing, coupling, filters, band_counts, band_offsets, band_basis):
    forward, inverse = spectral_tables()
    mode_local = filters.shape[3]
    blocks = lax.axis_size("polar")
    own_block = lax.axis_index("polar")
    inputs = (signal, cotangent)
    leading = jnp.einsum(
        "inc,npm->mpic",
        lax.all_to_all(inputs[0], "azimuth", split_axis=2, concat_axis=1, tiled=True),
        forward,
        preferred_element_type=jnp.float32,
    )
    trailing = jnp.einsum(
        "inc,mpn->mpic",
        lax.all_to_all(inputs[1], "azimuth", split_axis=2, concat_axis=1, tiled=True),
        inverse,
        preferred_element_type=jnp.float32,
    )
    stacked = jnp.stack([leading, trailing], axis=1).astype(jnp.bfloat16)
    both_spectra = lax.all_to_all(stacked, "azimuth", split_axis=0, concat_axis=4, tiled=True)
    rims = extended(both_spectra, (("polar", 3),), BLOCK)
    channels = signal.shape[2]
    zero_sum = jnp.zeros((mode_local, 2, BLOCK, channels), jnp.float32)
    slot_count = coupling.shape[1]

    def forward_basis(basis_index):

        def forward_slot(slot, running):
            used = band_basis[own_block, slot] == basis_index

            def forward_update(running):
                offset = band_offsets[own_block, slot]
                source = rows_of(rims, 0, (offset + 1) * BLOCK)
                coupled = jnp.einsum(
                    "rj,mpjc->mprc",
                    coupling[own_block, slot],
                    source,
                    preferred_element_type=jnp.float32,
                )
                return running + apply_filter(filters[own_block, slot], coupled, False)

            return lax.cond(used, forward_update, lambda kept: kept, running)

        return lax.fori_loop(0, band_counts[own_block], forward_slot, zero_sum).astype(jnp.bfloat16)

    basis_rounded = jnp.stack([forward_basis(index) for index in range(K)], axis=0)
    out_spectra = jnp.einsum(
        "kmpic,kcd->mpid", basis_rounded, mixing, preferred_element_type=jnp.float32
    ).astype(jnp.bfloat16)

    def backward_basis(basis_index):
        running = zero_sum
        for step_by in (-1, 0, 1):
            neighbour = own_block + step_by
            inside = (neighbour >= 0) & (neighbour < blocks)
            safe = jnp.clip(neighbour, 0, blocks - 1)
            source = rows_of(rims, 1, (step_by + 1) * BLOCK)
            count_there = band_counts[safe]

            def backward_slot(
                slot,
                running,
                safe=safe,
                inside=inside,
                source=source,
                count_there=count_there,
                step_by=step_by,
            ):
                used = (
                    inside
                    & (slot < count_there)
                    & (band_offsets[safe, slot] == -step_by)
                    & (band_basis[safe, slot] == basis_index)
                )

                def backward_update(running):
                    lifted = jnp.einsum(
                        "jr,mpjc->mprc",
                        coupling[safe, slot],
                        source,
                        preferred_element_type=jnp.float32,
                    )
                    return running + apply_filter(filters[safe, slot], lifted, True)

                return lax.cond(used, backward_update, lambda kept: kept, running)

            running = lax.fori_loop(0, slot_count, backward_slot, running)
        return running.astype(jnp.bfloat16)

    back_rounded = jnp.stack([backward_basis(index) for index in range(K)], axis=0)
    grad_spectra = jnp.einsum(
        "kmpjd,kcd->mpjc", back_rounded, mixing, preferred_element_type=jnp.float32
    ).astype(jnp.bfloat16)
    stacked = jnp.stack([out_spectra, grad_spectra], axis=1)
    piece = lax.all_to_all(stacked, "azimuth", split_axis=4, concat_axis=0, tiled=True)
    leading = jnp.einsum("mpic,mpn->inc", piece[:, 0], inverse, preferred_element_type=jnp.float32)
    trailing = jnp.einsum("mpjc,npm->jnc", piece[:, 1], forward, preferred_element_type=jnp.float32)
    columns = jnp.stack([leading, trailing], axis=0).astype(jnp.bfloat16)
    result = lax.all_to_all(columns, "azimuth", split_axis=2, concat_axis=3, tiled=True)
    return (result[0], result[1])


def solution(mesh):
    return jax.shard_map(
        per_device,
        mesh=mesh,
        in_specs=(
            P("polar", "azimuth", None),
            P("polar", "azimuth", None),
            P(),
            P(),
            P(None, None, None, "azimuth"),
            P(),
            P(),
            P(),
        ),
        out_specs=(P("polar", "azimuth", None), P("polar", "azimuth", None)),
        check_vma=False,
    )
```

profile of v0, /device:TPU:112, one launch (start us, length us, event | category | flops | bytes accessed | tf_op | source)
XLA Modules:
  0.0 1099.2 jit_solution(5299957490535361412)
XLA Ops:
  17.8 44.1 %all-to-all-done.1 = bf16[64,96,256]{1,0,2:T(8,128)(2,1)} async-done(((bf16[64,96,256]{1,0,2:T(8,128)(2,1)}), bf16[64,96,256]{1,0,2:T(8,128)(2,1)}, u32[]{:S(2)}, u32[]{:S(2)}) %all-to-all-start.1) | async-done | bytes 3145760 | tf_op jit(solution)/shard_map/all_to_all | solution.py:78
  61.9 17.1 %all-to-all-start = ((bf16[64,96,256]{1,0,2:T(8,128)(2,1)}), bf16[64,96,256]{1,0,2:T(8,128)(2,1)}, u32[]{:S(2)}, u32[]{:S(2)}) async-start(bf16[64,96,256]{1,0,2:T(8,128)(2,1)} %copy.49), calls=%async_computation | async-start | bytes 8388608 | tf_op jit(solution)/shard_map/all_to_all | solution.py:72
  91.6 12.3 %copy.54 = bf16[64,8,96,32]{2,1,0,3:T(8,128)(2,1)} copy(bf16[64,8,96,32]{2,0,3,1:T(8,128)(2,1)} %bitcast.80) | data formatting | bytes 6291456 | tf_op jit(solution)/shard_map/all_to_all | solution.py:78
  110.5 16.9 %all-to-all-done = bf16[64,96,256]{1,0,2:T(8,128)(2,1)} async-done(((bf16[64,96,256]{1,0,2:T(8,128)(2,1)}), bf16[64,96,256]{1,0,2:T(8,128)(2,1)}, u32[]{:S(2)}, u32[]{:S(2)}) %all-to-all-start) | async-done | bytes 3145760 | tf_op jit(solution)/shard_map/all_to_all | solution.py:72
  127.3 12.3 %copy.51 = bf16[64,8,96,32]{2,1,0,3:T(8,128)(2,1)} copy(bf16[64,8,96,32]{2,0,3,1:T(8,128)(2,1)} %bitcast.73) | data formatting | bytes 6291456 | tf_op jit(solution)/shard_map/all_to_all | solution.py:72
  159.2 18.5 %copy.55 = bf16[384,2,2,64,32]{3,4,2,1,0:T(8,128)(2,1)} copy(bf16[384,2,2,64,32]{0,3,4,2,1:T(8,128)(2,1)} %pad_maximum_fusion.1) | data formatting | bytes 12582912 | tf_op jit(solution)/shard_map/stack | solution.py:82
  177.7 13.8 %reshape.276 = bf16[8,2,196608]{2,1,0:T(2,128)(2,1)} reshape(bf16[384,2,2,32,64]{4,3,2,1,0:T(8,128)(2,1)} %bitcast.295) | data formatting | bytes 12582912
  191.4 83.4 %all_to_all.87 = bf16[8,2,196608]{2,1,0:T(2,128)(2,1)} all-to-all(bf16[8,2,196608]{2,1,0:T(2,128)(2,1)} %reshape.276), channel_id=1, replica_groups=mesh['polar'=16,'azimuth'=8] {'azimuth'}, dimensions={0} | all-to-all | bytes 12582912 | tf_op jit(solution)/shard_map/all_to_all | solution.py:83
  274.9 13.4 %reshape.277 = bf16[384,2,2,32,64]{4,3,2,1,0:T(8,128)(2,1)} reshape(bf16[8,2,196608]{2,1,0:T(2,128)(2,1)} %all_to_all.87) | data formatting | bytes 12582912
  288.3 11.5 %copy.57 = bf16[48,2,2,64,8,32]{3,5,4,2,1,0:T(8,128)(2,1)} copy(bf16[48,2,2,64,8,32]{3,5,2,1,0,4:T(8,128)(2,1)} %bitcast.296) | data formatting | bytes 12582912 | tf_op jit(solution)/shard_map/all_to_all | solution.py:83
  299.8 12.3 %copy.58 = bf16[48,2,2,64,256]{4,3,2,1,0:T(8,128)(2,1)} copy(bf16[48,2,2,64,256]{3,4,2,1,0:T(8,128)(2,1)} %bitcast.291) | data formatting | bytes 12582912 | tf_op jit(solution)/shard_map/all_to_all | solution.py:83
  331.8 53.1 %collective-permute-done = bf16[48,2,2,64,256]{4,3,2,1,0:T(8,128)(2,1)} collective-permute-done((bf16[48,2,2,64,256]{4,3,2,1,0:T(8,128)(2,1)}, bf16[48,2,2,64,256]{4,3,2,1,0:T(8,128)(2,1)}, u32[]{:S(2)}, u32[]{:S(2)}) %collective-permute-start) | collective-permute-done | bytes 6291488 | tf_op jit(solution)/shard_map/ppermute | solution.py:22
  392.3 29.8 %while.149 = (s32[]{:T(128)}, f32[48,2,64,256]{3,2,1,0:T(8,128)}, s32[]{:T(128)}, pred[]{:T(512)}, s32[16,6]{0,1:T(8,128)S(1)}, /*index=5*/s32[]{:T(128)}, s32[1...) while((s32[]{:T(128)}, f32[48,2,64,256]{3,2,1,0:T(8,128)}, ...), condition=%wide.region_23.24_spmd, body=%wide.region_20.23_spmd.sunk | while | flops 209190976 | bytes 40913096 | solution.py:150
  407.5 11.6 %conditional.21 = (f32[48,2,64,256]{3,2,1,0:T(8,128)}) conditional(s32[]{:T(128)} %convert_element_type.190, f32[48,2,64,256]{3,2,1,0:T(8,128)} %get-tuple-element.2967, (s32[]{:T(128)}, s32[]{:T(128)}, f32[16,6,2,48]{3,2,1,0:T(2,128)}, bf16[16,6,64,64]{2,3,1,0:T(8,128)(2,1)}, bf16[48,2,64,256]{3,2,1,0:T(8,128)(2,1)}, ...), branch_computations={%region_21.21_spmd, %region_22.22_spmd} | conditional | flops 209190960 | bytes 40912860 | solution.py:148
  422.1 29.1 %while.150 = (s32[]{:T(128)}, f32[48,2,64,256]{3,2,1,0:T(8,128)}, s32[]{:T(128)}, pred[]{:T(512)}, s32[16,6]{0,1:T(8,128)S(1)}, /*index=5*/s32[]{:T(128)}, s32[1...) while((s32[]{:T(128)}, f32[48,2,64,256]{3,2,1,0:T(8,128)}, ...), condition=%wide.region_27.28_spmd, body=%wide.region_24.27_spmd.sunk | while | flops 209190976 | bytes 40913104 | solution.py:150
  440.8 10.4 conditional.22
  455.2 28.9 %while.151 = (s32[]{:T(128)}, f32[48,2,64,256]{3,2,1,0:T(8,128)}, s32[]{:T(128)}, pred[]{:T(512)}, s32[16,6]{0,1:T(8,128)S(1)}, /*index=5*/s32[]{:T(128)}, s32[1...) while((s32[]{:T(128)}, f32[48,2,64,256]{3,2,1,0:T(8,128)}, ...), condition=%wide.region_31.32_spmd, body=%wide.region_28.31_spmd.sunk | while | flops 209190976 | bytes 40913104 | solution.py:150
  458.4 11.6 %conditional.23 = (f32[48,2,64,256]{3,2,1,0:T(8,128)}) conditional(s32[]{:T(128)} %convert_element_type.192, f32[48,2,64,256]{3,2,1,0:T(8,128)} %get-tuple-element.3043, (s32[]{:T(128)}, s32[]{:T(128)}, f32[16,6,2,48]{3,2,1,0:T(2,128)}, bf16[16,6,64,64]{2,3,1,0:T(8,128)(2,1)}, bf16[48,2,64,256]{3,2,1,0:T(8,128)(2,1)}, ...), branch_computations={%region_29.29_spmd, %region_30.30_spmd} | conditional | flops 209190960 | bytes 40912860 | solution.py:148
  492.4 31.8 %while.146 = (s32[]{:T(128)}, f32[48,2,64,256]{3,2,1,0:T(8,128)}, s32[]{:T(128)}, pred[]{:T(512)}, s32[16,6]{0,1:T(8,128)S(1)}, /*index=5*/s32[]{:T(128)}, s32[1...) while((s32[]{:T(128)}, f32[48,2,64,256]{3,2,1,0:T(8,128)}, ...), condition=%wide.region_11.12_spmd, body=%wide.region_8.11_spmd.sunk | while | flops 209190976 | bytes 40913104 | solution.py:150
  502.5 11.5 %conditional.18 = (f32[48,2,64,256]{3,2,1,0:T(8,128)}) conditional(s32[]{:T(128)} %convert_element_type.187, f32[48,2,64,256]{3,2,1,0:T(8,128)} %get-tuple-element.3082, (s32[]{:T(128)}, s32[]{:T(128)}, f32[16,6,2,48]{3,2,1,0:T(2,128)}, bf16[16,6,64,64]{2,3,1,0:T(8,128)(2,1)}, bf16[48,2,64,256]{3,2,1,0:T(8,128)(2,1)}, ...), branch_computations={%region_9.9_spmd, %region_10.10_spmd} | conditional | flops 209190960 | bytes 40912860 | solution.py:148
  524.2 30.6 %while.147 = (s32[]{:T(128)}, f32[48,2,64,256]{3,2,1,0:T(8,128)}, s32[]{:T(128)}, pred[]{:T(512)}, s32[16,6]{0,1:T(8,128)S(1)}, /*index=5*/s32[]{:T(128)}, s32[1...) while((s32[]{:T(128)}, f32[48,2,64,256]{3,2,1,0:T(8,128)}, ...), condition=%wide.region_15.16_spmd, body=%wide.region_12.15_spmd.sunk | while | flops 209190976 | bytes 40913096 | solution.py:150
  531.0 10.3 conditional.19
  554.8 31.7 %while.148 = (s32[]{:T(128)}, f32[48,2,64,256]{3,2,1,0:T(8,128)}, s32[]{:T(128)}, pred[]{:T(512)}, s32[16,6]{0,1:T(8,128)S(1)}, /*index=5*/s32[]{:T(128)}, s32[1...) while((s32[]{:T(128)}, f32[48,2,64,256]{3,2,1,0:T(8,128)}, ...), condition=%wide.region_19.20_spmd, body=%wide.region_16.19_spmd.sunk | while | flops 209190976 | bytes 40913104 | solution.py:150
  561.7 11.5 %conditional.20 = (f32[48,2,64,256]{3,2,1,0:T(8,128)}) conditional(s32[]{:T(128)} %convert_element_type.189, f32[48,2,64,256]{3,2,1,0:T(8,128)} %get-tuple-element.3157, (s32[]{:T(128)}, s32[]{:T(128)}, f32[16,6,2,48]{3,2,1,0:T(2,128)}, bf16[16,6,64,64]{2,3,1,0:T(8,128)(2,1)}, bf16[48,2,64,256]{3,2,1,0:T(8,128)(2,1)}, ...), branch_computations={%region_17.17_spmd, %region_18.18_spmd} | conditional | flops 209190960 | bytes 40912860 | solution.py:148
  591.5 11.9 %copy.61 = bf16[48,2,2,64,256]{3,4,2,1,0:T(8,128)(2,1)} copy(bf16[48,2,2,64,256]{4,3,2,1,0:T(8,128)(2,1)} %collective-permute-done.1) | data formatting | bytes 12582912 | tf_op jit(solution)/shard_map/ppermute | solution.py:24
  603.4 11.9 %copy.60 = bf16[48,2,2,64,256]{3,4,2,1,0:T(8,128)(2,1)} copy(bf16[48,2,2,64,256]{4,3,2,1,0:T(8,128)(2,1)} %collective-permute-done) | data formatting | bytes 12582912 | tf_op jit(solution)/shard_map/ppermute | solution.py:22
  615.4 26.9 %pad_maximum_fusion = bf16[48,2,2,192,256]{3,4,2,1,0:T(8,128)(2,1)} fusion(bf16[48,2,2,64,256]{3,4,2,1,0:T(8,128)(2,1)} %copy.61, bf16[48,2,2,64,256]{3,4,2,1,0:T(8,128)(2,1)} %bitcast.293, bf16[48,2,2,64,256]{3,4,2,1,0:T(8,128)(2,1)} %copy.60), kind=kLoop, calls=%fused_computation.86 | loop fusion | flops 56623104 | bytes 37748736 | tf_op jit(solution)/shard_map/concatenate | solution.py:20
  642.3 28.3 %copy.62 = bf16[48,2,2,192,256]{4,3,2,0,1:T(8,128)(2,1)} copy(bf16[48,2,2,192,256]{3,4,2,1,0:T(8,128)(2,1)} %pad_maximum_fusion) | data formatting | bytes 37748736 | tf_op jit(solution)/shard_map/while | solution.py:107
  674.1 51.5 %while.145 = (s32[]{:T(128)}, f32[48,2,64,256]{3,2,1,0:T(8,128)}, s32[]{:T(128)}, s32[16,6]{0,1:T(8,128)S(1)}, s32[]{:T(128)}, /*index=5*/s32[]{:T(128)}, f32[16...) while((s32[]{:T(128)}, f32[48,2,64,256]{3,2,1,0:T(8,128)}, ...), condition=%wide.region_7.8_spmd, body=%wide.region_4.7_spmd.sunk | while | flops 209190928 | bytes 40913192 | solution.py:107
  676.1 12.8 %conditional.17 = (f32[48,2,64,256]{3,2,1,0:T(8,128)}) conditional(s32[]{:T(128)} %bitcast.278, f32[48,2,64,256]{3,2,1,0:T(8,128)} %get-tuple-element.3197, (s32[]{:T(128)}, s32[]{:T(128)}, f32[16,6,2,48]{3,2,1,0:T(2,128)}, s32[16,6]{0,1:T(8,128)S(1)}, bf16[48,2,2,192,256]{4,3,2,0,1:T(8,128)(2,1)}, /*index=5*/bf16[16,6,64,64]{3,2,1,0:T(8,128)(2,1)}, ...), branch_computations={%region_5.5_spmd, %region_6.6_spmd} | conditional | flops 209190928 | bytes 40912936 | solution.py:105
  693.1 12.8 %conditional.17 = (f32[48,2,64,256]{3,2,1,0:T(8,128)}) conditional(s32[]{:T(128)} %bitcast.278, f32[48,2,64,256]{3,2,1,0:T(8,128)} %get-tuple-element.3197, (s32[]{:T(128)}, s32[]{:T(128)}, f32[16,6,2,48]{3,2,1,0:T(2,128)}, s32[16,6]{0,1:T(8,128)S(1)}, bf16[48,2,2,192,256]{4,3,2,0,1:T(8,128)(2,1)}, /*index=5*/bf16[16,6,64,64]{3,2,1,0:T(8,128)(2,1)}, ...), branch_computations={%region_5.5_spmd, %region_6.6_spmd} | conditional | flops 209190928 | bytes 40912936 | solution.py:105
  712.1 12.8 %conditional.17 = (f32[48,2,64,256]{3,2,1,0:T(8,128)}) conditional(s32[]{:T(128)} %bitcast.278, f32[48,2,64,256]{3,2,1,0:T(8,128)} %get-tuple-element.3197, (s32[]{:T(128)}, s32[]{:T(128)}, f32[16,6,2,48]{3,2,1,0:T(2,128)}, s32[16,6]{0,1:T(8,128)S(1)}, bf16[48,2,2,192,256]{4,3,2,0,1:T(8,128)(2,1)}, /*index=5*/bf16[16,6,64,64]{3,2,1,0:T(8,128)(2,1)}, ...), branch_computations={%region_5.5_spmd, %region_6.6_spmd} | conditional | flops 209190928 | bytes 40912936 | solution.py:105
  732.3 51.5 %while.144 = (s32[]{:T(128)}, f32[48,2,64,256]{3,2,1,0:T(8,128)}, s32[]{:T(128)}, s32[16,6]{0,1:T(8,128)S(1)}, s32[]{:T(128)}, /*index=5*/s32[]{:T(128)}, f32[16...) while((s32[]{:T(128)}, f32[48,2,64,256]{3,2,1,0:T(8,128)}, ...), condition=%wide.region_3.4_spmd, body=%wide.region_0.3_spmd.sunk | while | flops 209190928 | bytes 40913192 | solution.py:107
  736.4 12.8 %conditional.16 = (f32[48,2,64,256]{3,2,1,0:T(8,128)}) conditional(s32[]{:T(128)} %bitcast.277, f32[48,2,64,256]{3,2,1,0:T(8,128)} %get-tuple-element.3239, (s32[]{:T(128)}, s32[]{:T(128)}, f32[16,6,2,48]{3,2,1,0:T(2,128)}, s32[16,6]{0,1:T(8,128)S(1)}, bf16[48,2,2,192,256]{4,3,2,0,1:T(8,128)(2,1)}, /*index=5*/bf16[16,6,64,64]{3,2,1,0:T(8,128)(2,1)}, ...), branch_computations={%region_1.1_spmd, %region_2.2_spmd} | conditional | flops 209190928 | bytes 40912936 | solution.py:105
  753.3 12.8 %conditional.16 = (f32[48,2,64,256]{3,2,1,0:T(8,128)}) conditional(s32[]{:T(128)} %bitcast.277, f32[48,2,64,256]{3,2,1,0:T(8,128)} %get-tuple-element.3239, (s32[]{:T(128)}, s32[]{:T(128)}, f32[16,6,2,48]{3,2,1,0:T(2,128)}, s32[16,6]{0,1:T(8,128)S(1)}, bf16[48,2,2,192,256]{4,3,2,0,1:T(8,128)(2,1)}, /*index=5*/bf16[16,6,64,64]{3,2,1,0:T(8,128)(2,1)}, ...), branch_computations={%region_1.1_spmd, %region_2.2_spmd} | conditional | flops 209190928 | bytes 40912936 | solution.py:105
  768.2 12.8 %conditional.16 = (f32[48,2,64,256]{3,2,1,0:T(8,128)}) conditional(s32[]{:T(128)} %bitcast.277, f32[48,2,64,256]{3,2,1,0:T(8,128)} %get-tuple-element.3239, (s32[]{:T(128)}, s32[]{:T(128)}, f32[16,6,2,48]{3,2,1,0:T(2,128)}, s32[16,6]{0,1:T(8,128)S(1)}, bf16[48,2,2,192,256]{4,3,2,0,1:T(8,128)(2,1)}, /*index=5*/bf16[16,6,64,64]{3,2,1,0:T(8,128)(2,1)}, ...), branch_computations={%region_1.1_spmd, %region_2.2_spmd} | conditional | flops 209190928 | bytes 40912936 | solution.py:105
  795.6 26.8 %copy.72 = bf16[48,2,2,64,256]{3,2,0,1,4:T(2,128)(2,1)} copy(bf16[48,2,2,64,256]{4,3,2,0,1:T(8,128)(2,1)} %pad_maximum_fusion.2) | data formatting | bytes 12582912 | tf_op jit(solution)/shard_map/stack | solution.py:157
  822.4 13.8 %reshape.278 = bf16[8,2,196608]{2,1,0:T(2,128)(2,1)} reshape(bf16[256,2,48,2,64]{4,3,2,1,0:T(2,128)(2,1)} %bitcast.297) | data formatting | bytes 12582912
  836.2 45.2 %all_to_all.88 = bf16[8,2,196608]{2,1,0:T(2,128)(2,1)} all-to-all(bf16[8,2,196608]{2,1,0:T(2,128)(2,1)} %reshape.278), channel_id=1, replica_groups=mesh['polar'=16,'azimuth'=8] {'azimuth'}, dimensions={0} | all-to-all | bytes 12582912 | tf_op jit(solution)/shard_map/all_to_all | solution.py:158
  881.4 13.4 %reshape.279 = bf16[256,2,48,2,64]{4,3,2,1,0:T(2,128)(2,1)} reshape(bf16[8,2,196608]{2,1,0:T(2,128)(2,1)} %all_to_all.88) | data formatting | bytes 12582912
  894.8 13.5 %copy.73 = bf16[48,2,2,64,256]{3,4,2,1,0:T(8,128)(2,1)} copy(bf16[48,2,2,64,256]{3,2,0,1,4:T(2,128)(2,1)} %bitcast.298) | data formatting | bytes 12582912 | tf_op jit(solution)/shard_map/all_to_all | solution.py:158
  908.3 24.6 %copy.100 = bf16[8,48,2,2,64,32]{1,0,4,3,5,2:T(8,128)(2,1)} copy(bf16[8,48,2,2,64,32]{4,5,0,3,2,1:T(8,128)(2,1)} %bitcast.294) | data formatting | bytes 12582912 | tf_op jit(solution)/shard_map/all_to_all | solution.py:158
  932.9 21.9 %reshape.275 = bf16[384,2,2,64,32]{0,3,2,4,1:T(8,128)(2,1)} reshape(bf16[8,48,2,2,64,32]{1,0,4,3,5,2:T(8,128)(2,1)} %copy.100) | data formatting | bytes 12582912 | tf_op jit(solution)/shard_map/all_to_all | solution.py:158
  965.8 18.5 %copy.77 = bf16[2,64,768,32]{1,3,0,2:T(8,128)(2,1)} copy(bf16[2,64,768,32]{2,1,3,0:T(8,128)(2,1)} %pad_maximum_fusion.3) | data formatting | bytes 12582912 | tf_op jit(solution)/shard_map/stack | solution.py:161
  984.2 13.8 %reshape.280 = bf16[8,2,196608]{2,1,0:T(2,128)(2,1)} reshape(bf16[768,2,32,64]{3,2,1,0:T(8,128)(2,1)} %bitcast.299) | data formatting | bytes 12582912
  998.0 45.2 %all_to_all.89 = bf16[8,2,196608]{2,1,0:T(2,128)(2,1)} all-to-all(bf16[8,2,196608]{2,1,0:T(2,128)(2,1)} %reshape.280), channel_id=1, replica_groups=mesh['polar'=16,'azimuth'=8] {'azimuth'}, dimensions={0} | all-to-all | bytes 12582912 | tf_op jit(solution)/shard_map/all_to_all | solution.py:162
  1043.2 13.4 %reshape.281 = bf16[768,2,32,64]{3,2,1,0:T(8,128)(2,1)} reshape(bf16[8,2,196608]{2,1,0:T(2,128)(2,1)} %all_to_all.89) | data formatting | bytes 12582912
  1056.6 23.2 %copy.78 = bf16[2,64,8,96,32]{3,4,2,1,0:T(8,128)(2,1)} copy(bf16[2,64,8,96,32]{1,4,0,3,2:T(8,128)(2,1)} %bitcast.300) | data formatting | bytes 12582912 | tf_op jit(solution)/shard_map/all_to_all | solution.py:162
  (257 shorter events, 344.5 us)
Async XLA Ops:
  0.6 786.6 %copy-start = (bf16[2,256,256]{2,1,0:T(8,128)(2,1)S(1)}, bf16[2,256,256]{2,1,0:T(8,128)(2,1)}, u32[]{:S(2)}) copy-start(bf16[2,256,256]{2,1,0:T(8,128)(2,1)} %param.42) | copy-start | bytes 786436
  7.1 5.3 copy-start.2
  7.1 54.8 %all-to-all-start.1 = ((bf16[64,96,256]{1,0,2:T(8,128)(2,1)}), bf16[64,96,256]{1,0,2:T(8,128)(2,1)}, u32[]{:S(2)}, u32[]{:S(2)}) async-start(bf16[64,96,256]{1,0,2:T(8,128)(2,1)} %copy.52), calls=%async_computation.1 | async-start | bytes 8388608 | tf_op jit(solution)/shard_map/all_to_all | solution.py:78
  61.9 65.4 %all-to-all-start = ((bf16[64,96,256]{1,0,2:T(8,128)(2,1)}), bf16[64,96,256]{1,0,2:T(8,128)(2,1)}, u32[]{:S(2)}, u32[]{:S(2)}) async-start(bf16[64,96,256]{1,0,2:T(8,128)(2,1)} %copy.49), calls=%async_computation | async-start | bytes 8388608 | tf_op jit(solution)/shard_map/all_to_all | solution.py:72
  79.0 73.7 %copy-start.15 = (f32[384]{0:T(512)}, f32[384]{0:T(512)S(1)}, u32[]{:S(2)}) copy-start(f32[384]{0:T(512)S(1)} %select_multiply_fusion) | copy-start | bytes 4612
  147.7 5.0 copy-start.6
  147.7 5.0 copy-start.8
  299.8 18.0 %copy-start.5 = (bf16[16,6,64,64]{3,2,1,0:T(8,128)(2,1)S(1)}, bf16[16,6,64,64]{3,2,1,0:T(8,128)(2,1)}, u32[]{:S(2)}) copy-start(bf16[16,6,64,64]{3,2,1,0:T(8,128)(2,1)} %param.43) | copy-start | bytes 2359300
  312.2 7.5 copy-start.14
  312.2 72.7 %collective-permute-start = (bf16[48,2,2,64,256]{4,3,2,1,0:T(8,128)(2,1)}, bf16[48,2,2,64,256]{4,3,2,1,0:T(8,128)(2,1)}, u32[]{:S(2)}, u32[]{:S(2)}) collective-permute-start(bf16[48,2,2,64,256]{4,3,2,1,0:T(8,128)(2,1)} %copy.58), channel_id=1, source_target_pairs={{0,8},{8,16},{16,24},{24,32},{32,40},{40,48},{48,56},{56,64},{64,7... | collective-permute-start | bytes 18874376 | tf_op jit(solution)/shard_map/ppermute | solution.py:22
  314.2 137.0 %collective-permute-start.1 = (bf16[48,2,2,64,256]{4,3,2,1,0:T(8,128)(2,1)}, bf16[48,2,2,64,256]{4,3,2,1,0:T(8,128)(2,1)}, u32[]{:S(2)}, u32[]{:S(2)}) collective-permute-start(bf16[48,2,2,64,256]{4,3,2,1,0:T(8,128)(2,1)} %copy.58), channel_id=1, source_target_pairs={{8,0},{16,8},{24,16},{32,24},{40,32},{48,40},{56,48},{64,56},{72,6... | collective-permute-start | bytes 18874376 | tf_op jit(solution)/shard_map/ppermute | solution.py:24
  388.9 3.5 copy-start.12
  388.9 3.5 copy-start.13
  783.8 3.7 copy-start.3
  783.8 4.7 copy-start.4
  932.9 21.9 %copy-start.10 = (bf16[768,1,384]{2,0,1:T(8,128)(2,1)S(1)}, bf16[768,1,384]{2,0,1:T(8,128)(2,1)}, u32[]{:S(2)}) copy-start(bf16[768,1,384]{2,0,1:T(8,128)(2,1)} %get-tuple-element.2462) | copy-start | bytes 1769476
  932.9 21.9 %copy-start.11 = (bf16[768,1,384]{2,0,1:T(8,128)(2,1)S(1)}, bf16[768,1,384]{2,0,1:T(8,128)(2,1)}, u32[]{:S(2)}) copy-start(bf16[768,1,384]{2,0,1:T(8,128)(2,1)} %get-tuple-element.2463) | copy-start | bytes 1769476
  954.8 4.7 copy-start.1
  954.8 4.7 copy-start.7
  954.8 4.7 copy-start.9
  954.8 4.7 copy-start.16
where the time goes:
time: 1120 us; the launch traced here: 1100 us
  local copies, waits for them, and re-layouts  477 us (43%)
  blocking collectives  174 us (16%)
  other arithmetic  160 us (14%)
  waiting for transfers between devices  114 us (10%)
  loops' own time  92.6 us (8%)
  matrix products  52.1 us (5%)
  starting transfers between devices  28.1 us (3%)
    unnamed x44, local copies, waits for them, and re-layouts  107 us
    all_to_all x1, blocking collectives, per_device(): lax.all_to_all(stacked, 'azimuth', split_axis=0, concat_axis=4, tiled=True)  83.4 us
    another operation x6, loops' own time, backward_basis(): running = lax.fori_loop(0, slot_count, backward_slot, running)  69.9 us
    all_to_all x3, local copies, waits for them, and re-layouts, per_device(): lax.all_to_all(stacked, 'azimuth', split_axis=4, concat_axis=0, tiled=True)  60 us
    ppermute x1, waiting for transfers between devices, extended(): lax.ppermute(tail, axis, [(i, (i + 1) % count) for i in range(ends)])  53.1 us
    all_to_all x1, blocking collectives, per_device(): lax.all_to_all(columns, 'azimuth', split_axis=2, concat_axis=3, tiled=True)  45.2 us
    all_to_all x1, blocking collectives, per_device(): lax.all_to_all(stacked, 'azimuth', split_axis=4, concat_axis=0, tiled=True)  45.2 us
    all_to_all x1, waiting for transfers between devices, per_device(): lax.all_to_all(inputs[1], 'azimuth', split_axis=2, concat_axis=1, tiled=T...  44.1 us
  transfers between devices with their start and end apart: 4, of which 3 were waited for; matrix products, arithmetic and copies ran while one was open for 9% of the time, Pallas kernels for 0%

commit v1 on v0

v1 whole, which is shorter than its diff:
```python
import math

import jax
import jax.numpy as jnp
from jax import lax
from jax.experimental import pallas as pl
from jax.experimental.pallas import tpu as pltpu
from jax.sharding import PartitionSpec as P

NLON = 768
M = 384
K = 2
BLOCK = 64
PARTS = 8
LON = NLON // PARTS
CHANNELS = 256
SUB = 16
HALVES = 2
TILES = BLOCK // SUB
F32 = jnp.float32
BF16 = jnp.bfloat16


def spectral_tables():
    longitude = jnp.arange(NLON, dtype=jnp.int32)
    wavenumber = jnp.arange(M, dtype=jnp.int32)
    product_mod = wavenumber[:, None] * longitude[None, :] % NLON
    phase_angle = product_mod.astype(F32) * (2.0 * math.pi / NLON)
    table = jnp.concatenate([jnp.cos(phase_angle), -jnp.sin(phase_angle)], axis=0)
    weight = jnp.where(wavenumber == 0, 1.0, 2.0).astype(F32) / NLON
    weight = jnp.concatenate([weight, weight])
    forward = table.astype(BF16)
    inverse = (table * weight[:, None]).astype(BF16)
    return forward, inverse


def swap_order():
    index = jnp.arange(SUB * SUB, dtype=jnp.int32)
    partner = index % SUB * SUB + index // SUB
    return (index[None, :] == partner[:, None]).astype(BF16)


def butterfly(parts):
    parts = list(parts)
    lane = lax.broadcasted_iota(jnp.int32, parts[0].shape, 1)
    for bit in (1, 2, 4):
        shift = SUB * bit
        low = (lane & shift) == 0
        for place in range(8):
            if place & bit:
                continue
            first, second = parts[place], parts[place | bit]
            parts[place] = jnp.where(low, first, pltpu.roll(second, shift, 1))
            parts[place | bit] = jnp.where(low, pltpu.roll(first, 128 - shift, 1), second)
    return parts


def pack_kernel(x_ref, *out_refs):
    for v in range(2):
        for w in range(2):
            moved = butterfly(
                [x_ref[8 * w + e, :, 128 * v : 128 * v + 128].astype(F32) for e in range(8)]
            )
            for place in range(8):
                group = 8 * v + place
                out_refs[group % 2][group // 2, 0, :, 128 * w : 128 * w + 128] = moved[
                    place
                ].astype(BF16)


def pack(x):
    step = 32
    return pl.pallas_call(
        pack_kernel,
        grid=(TILES, LON // step),
        in_specs=[pl.BlockSpec((SUB, step, CHANNELS), lambda t, n: (t, n, 0))],
        out_specs=[
            pl.BlockSpec((PARTS, 1, step, CHANNELS), lambda t, n: (0, t, n, 0))
            for _ in range(HALVES)
        ],
        out_shape=[
            jax.ShapeDtypeStruct((PARTS, TILES, LON, CHANNELS), BF16) for _ in range(HALVES)
        ],
        cost_estimate=pl.CostEstimate(flops=0, bytes_accessed=6_300_000, transcendentals=0),
        name="pack",
    )(x)


def to_modes_kernel(t_ref, p_ref, x_ref, o_ref):
    x = x_ref[...].reshape(NLON, CHANNELS)
    spectra = jnp.dot(t_ref[...], x, preferred_element_type=F32).astype(BF16)
    turned = lax.dot_general(
        p_ref[...], spectra, (((1,), (1,)), ((), ())), preferred_element_type=F32
    )
    o_ref[...] = turned.astype(BF16).reshape(SUB, SUB, NLON)


def to_modes(table, order, x):
    return pl.pallas_call(
        to_modes_kernel,
        grid=(TILES,),
        in_specs=[
            pl.BlockSpec((NLON, NLON), lambda t: (0, 0)),
            pl.BlockSpec((SUB * SUB, SUB * SUB), lambda t: (0, 0)),
            pl.BlockSpec((PARTS, 1, LON, CHANNELS), lambda t: (0, t, 0, 0)),
        ],
        out_specs=pl.BlockSpec((SUB, SUB, NLON), lambda t: (0, t, 0)),
        out_shape=jax.ShapeDtypeStruct((SUB, BLOCK, NLON), BF16),
        cost_estimate=pl.CostEstimate(
            flops=2 * NLON * NLON * 1024, bytes_accessed=4_500_000, transcendentals=0
        ),
        name="to_modes",
    )(table, order, x)


def couple_kernel(a_ref, f_ref, l_ref, m_ref, r_ref, o_ref):
    for c in range(m_ref.shape[0]):
        for start in range(0, M, 128):
            real = [None] * K
            imag = [None] * K
            for side, s_ref in enumerate((l_ref, m_ref, r_ref)):
                source = jnp.concatenate(
                    [
                        s_ref[c, :, start : start + 128],
                        s_ref[c, :, M + start : M + start + 128],
                    ],
                    axis=1,
                )
                mixed = jnp.dot(a_ref[side], source, preferred_element_type=F32)
                for k in range(K):
                    row = 2 * (3 * k + side)
                    f_real = f_ref[row : row + 1, start : start + 128]
                    f_imag = f_ref[row + 1 : row + 2, start : start + 128]
                    c_real = mixed[BLOCK * k : BLOCK * (k + 1), :128]
                    c_imag = mixed[BLOCK * k : BLOCK * (k + 1), 128:]
                    t_real = f_real * c_real - f_imag * c_imag
                    t_imag = f_real * c_imag + f_imag * c_real
                    real[k] = t_real if side == 0 else real[k] + t_real
                    imag[k] = t_imag if side == 0 else imag[k] + t_imag
            for k in range(K):
                o_ref[k, c, :, start : start + 128] = real[k].astype(BF16)
                o_ref[k, c, :, M + start : M + start + 128] = imag[k].astype(BF16)


def couple(maps, filters, left, own, right):
    step = 4
    spec = pl.BlockSpec((step, BLOCK, NLON), lambda c: (c, 0, 0))
    return pl.pallas_call(
        couple_kernel,
        grid=(SUB // step,),
        in_specs=[
            pl.BlockSpec((3, K * BLOCK, BLOCK), lambda c: (0, 0, 0)),
            pl.BlockSpec((12, M), lambda c: (0, 0)),
            spec,
            spec,
            spec,
        ],
        out_specs=pl.BlockSpec((K, step, BLOCK, NLON), lambda c: (0, c, 0, 0)),
        out_shape=jax.ShapeDtypeStruct((K, SUB, BLOCK, NLON), BF16),
        cost_estimate=pl.CostEstimate(
            flops=4 * 2 * 3 * SUB * 128 * BLOCK * NLON,
            bytes_accessed=8_000_000,
            transcendentals=0,
        ),
        name="couple",
    )(maps, filters, left, own, right)


def to_longitudes_kernel(t_ref, p_ref, b_ref, o_ref):
    sums = b_ref[...].reshape(SUB * SUB, NLON)
    grid = lax.dot_general(
        t_ref[...], sums, (((1,), (1,)), ((), ())), preferred_element_type=F32
    ).astype(BF16)
    turned = jnp.dot(grid, p_ref[...], preferred_element_type=F32).astype(BF16)
    o_ref[...] = turned.reshape(PARTS, 1, 1, LON, CHANNELS)


def to_longitudes(table, order, sums):
    return pl.pallas_call(
        to_longitudes_kernel,
        grid=(K, TILES),
        in_specs=[
            pl.BlockSpec((NLON, NLON), lambda k, t: (0, 0)),
            pl.BlockSpec((SUB * SUB, SUB * SUB), lambda k, t: (0, 0)),
            pl.BlockSpec((1, SUB, SUB, NLON), lambda k, t: (k, 0, t, 0)),
        ],
        out_specs=pl.BlockSpec((PARTS, 1, 1, LON, CHANNELS), lambda k, t: (0, k, t, 0, 0)),
        out_shape=jax.ShapeDtypeStruct((PARTS, K, TILES, LON, CHANNELS), BF16),
        cost_estimate=pl.CostEstimate(
            flops=2 * NLON * NLON * 2048, bytes_accessed=7_500_000, transcendentals=0
        ),
        name="to_longitudes",
    )(table, order, sums)


def mix_kernel(turn, w_ref, *refs):
    halves, o_ref = refs[:-1], refs[-1]
    step = o_ref.shape[1]
    total = None
    for k in range(K):
        rows = [[None, None] for _ in range(SUB)]
        for v in range(2):
            for w in range(2):
                moved = butterfly(
                    [
                        halves[(8 * v + place) % 2][
                            (8 * v + place) // 2, k, 0, :, 128 * w : 128 * w + 128
                        ].astype(F32)
                        for place in range(8)
                    ]
                )
                for e in range(8):
                    rows[8 * w + e][v] = moved[e].astype(BF16)
        x = jnp.concatenate([jnp.concatenate(row, axis=1) for row in rows], axis=0)
        term = lax.dot_general(
            x, w_ref[k], (((1,), (1 if turn else 0,)), ((), ())), preferred_element_type=F32
        )
        total = term if total is None else total + term
    o_ref[...] = total.astype(BF16).reshape(SUB, step, CHANNELS)


def mix(mixing, halves, turn):
    step = 32
    return pl.pallas_call(
        lambda *refs: mix_kernel(turn, *refs),
        grid=(TILES, LON // step),
        in_specs=[pl.BlockSpec((K, CHANNELS, CHANNELS), lambda t, n: (0, 0, 0))]
        + [
            pl.BlockSpec((PARTS, K, 1, step, CHANNELS), lambda t, n: (0, 0, t, n, 0))
            for _ in range(HALVES)
        ],
        out_specs=pl.BlockSpec((SUB, step, CHANNELS), lambda t, n: (t, n, 0)),
        out_shape=jax.ShapeDtypeStruct((BLOCK, LON, CHANNELS), BF16),
        cost_estimate=pl.CostEstimate(
            flops=2 * 64 * 96 * 512 * 256, bytes_accessed=9_500_000, transcendentals=0
        ),
        name="mix",
    )(mixing, *halves)


def exchange(x):
    return lax.all_to_all(x, "azimuth", split_axis=0, concat_axis=0, tiled=True)


def neighbours(x):
    count = lax.axis_size("polar")
    return (
        lax.ppermute(x, "polar", [(i, i + 1) for i in range(count - 1)]),
        lax.ppermute(x, "polar", [(i + 1, i) for i in range(count - 1)]),
    )


def dense_tables(coupling, filters, band_counts, band_offsets, band_basis):
    blocks = lax.axis_size("polar")
    own = lax.axis_index("polar")
    slots = coupling.shape[1]
    maps = {}
    gains = {}
    for step in (-1, 0, 1):
        there = own + step
        inside = (there >= 0) & (there < blocks)
        safe = jnp.clip(there, 0, blocks - 1)
        used = inside & (jnp.arange(slots) < band_counts[safe])
        for k in range(K):
            for offset in (-1, 0, 1):
                if step != 0 and offset != -step:
                    continue
                pick = used & (band_offsets[safe] == offset) & (band_basis[safe] == k)
                maps[step, k, offset] = jnp.sum(
                    jnp.where(pick[:, None, None], coupling[safe], 0).astype(F32), axis=0
                ).astype(BF16)
                gains[step, k, offset] = jnp.sum(
                    jnp.where(pick[:, None, None], filters[safe], 0.0), axis=0
                )
    ahead_maps = jnp.stack(
        [jnp.concatenate([maps[0, k, o] for k in range(K)], axis=0) for o in (-1, 0, 1)]
    )
    back_maps = jnp.stack(
        [jnp.concatenate([maps[s, k, -s].T for k in range(K)], axis=0) for s in (-1, 0, 1)]
    )
    ahead = jnp.stack([gains[0, k, o] for k in range(K) for o in (-1, 0, 1)])
    back = jnp.stack([gains[s, k, -s] for k in range(K) for s in (-1, 0, 1)])
    back = back * jnp.array([1.0, -1.0], F32)[None, :, None]
    local = jnp.concatenate([ahead, back]).reshape(1, 9, 128)
    every = exchange(jnp.broadcast_to(local, (PARTS, 9, 128)))
    every = every.reshape(PARTS, 24, M // PARTS).transpose(1, 0, 2).reshape(24, M)
    return ahead_maps, back_maps, every[:12], every[12:]


def per_device(signal, cotangent, mixing, coupling, filters, band_counts, band_offsets, band_basis):
    forward, inverse = spectral_tables()
    order = swap_order()
    ahead_maps, back_maps, ahead_gain, back_gain = dense_tables(
        coupling, filters, band_counts, band_offsets, band_basis
    )
    arrived = []
    for x in (signal, cotangent):
        arrived.append([exchange(part) for part in pack(x)])
    results = []
    for parts, table, back_table, maps, gain, turn in (
        (arrived[0], forward, inverse.T, ahead_maps, ahead_gain, False),
        (arrived[1], inverse, forward.T, back_maps, back_gain, True),
    ):
        returned = []
        for part in parts:
            spectra = to_modes(table, order, part)
            left, right = neighbours(spectra)
            sums = couple(maps, gain, left, spectra, right)
            returned.append(exchange(to_longitudes(back_table, order, sums)))
        results.append(mix(mixing, returned, turn))
    return tuple(results)


def solution(mesh):
    return jax.shard_map(
        per_device,
        mesh=mesh,
        in_specs=(
            P("polar", "azimuth", None),
            P("polar", "azimuth", None),
            P(),
            P(),
            P(None, None, None, "azimuth"),
            P(),
            P(),
            P(),
        ),
        out_specs=(P("polar", "azimuth", None), P("polar", "azimuth", None)),
        check_vma=False,
    )
```

time: 1120 us -> 406 us (0.36)
  the two profiles are of different devices: /device:TPU:112 before, /device:TPU:30 now
where the time goes in v1:
time: 406 us; the launch traced here: 403 us
  waiting for transfers between devices  140 us (34%)
  Pallas kernels  138 us (34%)
  starting transfers between devices  72.8 us (18%)
  blocking collectives  23.9 us (6%)
  other arithmetic  16.1 us (4%)
  local copies, waits for them, and re-layouts  11.4 us (3%)
    ppermute x4, waiting for transfers between devices, neighbours(): lax.ppermute(x, 'polar', [(i + 1, i) for i in range(count - 1)])  95.4 us
    all_to_all x8, starting transfers between devices, exchange(): return lax.all_to_all(x, 'azimuth', split_axis=0, concat_axis=0, tiled=True)  47.6 us
    pallas_call x4, Pallas kernels, to_longitudes(): pl.pallas_call(to_longitudes_kernel, grid=(K, TILES), in_specs=[pl.BlockS...  37.5 us
    pallas_call x2, Pallas kernels, mix(): pl.pallas_call(lambda *refs: mix_kernel(turn, *refs), grid=(TILES, LON //...  31.3 us
    ppermute x4, waiting for transfers between devices, neighbours(): lax.ppermute(x, 'polar', [(i, i + 1) for i in range(count - 1)])  27.6 us
    pallas_call x4, Pallas kernels, couple(): pl.pallas_call(couple_kernel, grid=(SUB // step,), in_specs=[pl.BlockSpec...  25.1 us
    all_to_all x1, blocking collectives, exchange(): return lax.all_to_all(x, 'azimuth', split_axis=0, concat_axis=0, tiled=True)  23.9 us
    pallas_call x4, Pallas kernels, to_modes(): pl.pallas_call(to_modes_kernel, grid=(TILES,), in_specs=[pl.BlockSpec((NL...  22.5 us
  transfers between devices with their start and end apart: 16, of which 8 were waited for; matrix products, arithmetic and copies ran while one was open for 4% of the time, Pallas kernels for 30%

profile of v1, /device:TPU:30, one launch (start us, length us, event | category | flops | bytes accessed | tf_op | source)
XLA Modules:
  0.0 403.1 jit_solution(5070591520695417315)
XLA Ops:
  0.6 1.4 fusion.39
  2.1 1.2 fusion.29
  8.0 5.7 %all-to-all-start = ((f32[8,9,128]{2,1,0:T(8,128)}), f32[8,9,128]{2,1,0:T(8,128)S(1)}, u32[]{:S(2)}, u32[]{:S(2)}) async-start(f32[8,9,128]{2,1,0:T(8,128)} %broadcast_in_dim.194), calls=%async_computation | async-start | bytes 131072 | tf_op jit(solution)/shard_map/all_to_all | solution.py:242
  13.6 10.7 %pack.2 = (bf16[8,4,96,256]{3,2,1,0:T(8,128)(2,1)}, bf16[8,4,96,256]{3,2,1,0:T(8,128)(2,1)}) custom-call(bf16[64,96,256]{2,1,0:T(8,128)(2,1)} %x_ref.2), custom_call_target="tpu_custom_call" | custom-call | bytes 6300000 | tf_op jit(solution)/shard_map/pack/pallas_call | solution.py:73
  24.4 23.9 %all_to_all.45.x_ref = bf16[8,4,96,256]{3,2,1,0:T(8,128)(2,1)} all-to-all(bf16[8,4,96,256]{3,2,1,0:T(8,128)(2,1)} %get-tuple-element.6), channel_id=1, replica_groups=mesh['polar'=16,'azimuth'=8] {'azimuth'}, dimensions={0} | all-to-all | bytes 3145728 | tf_op jit(solution)/shard_map/all_to_all | solution.py:242
  48.3 6.2 %all-to-all-start.3 = ((bf16[8,4,96,256]{3,2,1,0:T(8,128)(2,1)}), bf16[8,4,96,256]{3,2,1,0:T(8,128)(2,1)S(1)}, u32[]{:S(2)}, u32[]{:S(2)}) async-start(bf16[8,4,96,256]{3,2,1,0:T(8,128)(2,1)} %get-tuple-element.7), calls=%async_computation.3 | async-start | bytes 3145728 | tf_op jit(solution)/shard_map/all_to_all | solution.py:242
  54.5 10.8 %pack.3 = (bf16[8,4,96,256]{3,2,1,0:T(8,128)(2,1)}, bf16[8,4,96,256]{3,2,1,0:T(8,128)(2,1)}) custom-call(bf16[64,96,256]{2,1,0:T(8,128)(2,1)} %x_ref.3), custom_call_target="tpu_custom_call" | custom-call | bytes 6300000 | tf_op jit(solution)/shard_map/pack/pallas_call | solution.py:73
  65.3 6.7 %all-to-all-done.3.x_ref = bf16[8,4,96,256]{3,2,1,0:T(8,128)(2,1)S(1)} async-done(((bf16[8,4,96,256]{3,2,1,0:T(8,128)(2,1)}), bf16[8,4,96,256]{3,2,1,0:T(8,128)(2,1)S(1)}, u32[]{:S(2)}, u32[]{:S(2)}) %all-to-all-start.3) | async-done | bytes 1572896 | tf_op jit(solution)/shard_map/all_to_all | solution.py:242
  73.1 6.9 %all-to-all-start.5 = ((bf16[8,4,96,256]{3,2,1,0:T(8,128)(2,1)}), bf16[8,4,96,256]{3,2,1,0:T(8,128)(2,1)}, u32[]{:S(2)}, u32[]{:S(2)}) async-start(bf16[8,4,96,256]{3,2,1,0:T(8,128)(2,1)} %get-tuple-element.8), calls=%async_computation.5 | async-start | bytes 3145728 | tf_op jit(solution)/shard_map/all_to_all | solution.py:242
  80.0 4.8 %sine_negate_fusion = (f32[384,768]{0,1:T(8,128)S(1)}, f32[384,768]{0,1:T(8,128)S(1)}) fusion(), kind=kLoop, calls=%fused_computation.6 | loop fusion | flops 2949120 | bytes 2359296 | tf_op jit(solution)/shard_map/neg | solution.py:29
  84.9 1.5 copy.26.t_ref
  87.2 5.6 %to_modes.5.m_ref = bf16[16,64,768]{2,1,0:T(8,128)(2,1)} custom-call(bf16[768,768]{1,0:T(8,128)(2,1)} %copy.26.t_ref, bf16[256,256]{1,0:T(8,128)(2,1)} %fusion.7.p_ref, bf16[8,4,96,256]{3,2,1,0:T(8,128)(2,1)} %copy-done.2), custom_call_target="tpu_custom_call" | custom-call | flops 1207959552 | bytes 4500000 | tf_op jit(solution)/shard_map/to_modes/pallas_call | solution.py:99
  92.9 5.7 %collective-permute-start.3 = (bf16[16,64,768]{2,1,0:T(8,128)(2,1)}, bf16[16,64,768]{2,1,0:T(8,128)(2,1)}, u32[]{:S(2)}, u32[]{:S(2)}) collective-permute-start(bf16[16,64,768]{2,1,0:T(8,128)(2,1)} %to_modes.5.m_ref), channel_id=1, source_target_pairs={{8,0},{16,8},{24,16},{32,24},{40,32},{48,40},{56,48},{64,56},{72,6... | collective-permute-start | bytes 4718600 | tf_op jit(solution)/shard_map/ppermute | solution.py:249
  98.5 1.9 collective-permute-start.2
  100.6 2.0 fusion.10
  103.1 5.7 %all-to-all-start.7 = ((bf16[8,4,96,256]{3,2,1,0:T(8,128)(2,1)}), bf16[8,4,96,256]{3,2,1,0:T(8,128)(2,1)}, u32[]{:S(2)}, u32[]{:S(2)}) async-start(bf16[8,4,96,256]{3,2,1,0:T(8,128)(2,1)} %get-tuple-element.9), calls=%async_computation.7 | async-start | bytes 3145728 | tf_op jit(solution)/shard_map/all_to_all | solution.py:242
  112.1 19.4 %collective-permute-done.3.r_ref = bf16[16,64,768]{2,1,0:T(8,128)(2,1)} collective-permute-done((bf16[16,64,768]{2,1,0:T(8,128)(2,1)}, bf16[16,64,768]{2,1,0:T(8,128)(2,1)}, u32[]{:S(2)}, u32[]{:S(2)}) %collective-permute-start.3) | collective-permute-done | bytes 1572896 | tf_op jit(solution)/shard_map/ppermute | solution.py:249
  131.5 7.4 %collective-permute-done.2.l_ref = bf16[16,64,768]{2,1,0:T(8,128)(2,1)} collective-permute-done((bf16[16,64,768]{2,1,0:T(8,128)(2,1)}, bf16[16,64,768]{2,1,0:T(8,128)(2,1)}, u32[]{:S(2)}, u32[]{:S(2)}) %collective-permute-start.2) | collective-permute-done | bytes 1572896 | tf_op jit(solution)/shard_map/ppermute | solution.py:248
  138.9 6.3 %couple.5.b_ref = bf16[2,16,64,768]{3,2,1,0:T(8,128)(2,1)} custom-call(bf16[3,128,64]{2,1,0:T(8,128)(2,1)} %pad_maximum_fusion.1.a_ref, f32[12,384]{1,0:T(8,128)} %slice.13.f_ref, bf16[16,64,768]{2,1,0:T(8,128)(2,1)} %collective-permute-done.2.l_ref, bf16[16,64,768]{2,1,0:T(8,128)(2,1)} %to_modes.5.m_ref, bf16[16,64,768]{2,1,0:T(8,128)(2,1)} %collective-permute-done.3.r_ref), custom_call_target="tpu_custom_call" | custom-call | flops 2415919104 | bytes 8000000 | tf_op jit(solution)/shard_map/couple/pallas_call | solution.py:148
  145.2 9.4 %to_longitudes.5 = bf16[8,2,4,96,256]{4,3,2,1,0:T(8,128)(2,1)} custom-call(bf16[768,768]{1,0:T(8,128)(2,1)} %bitcast.113, bf16[256,256]{1,0:T(8,128)(2,1)} %fusion.7.p_ref, bf16[2,16,64,768]{3,2,1,0:T(8,128)(2,1)} %couple.5.b_ref), custom_call_target="tpu_custom_call" | custom-call | flops 2415919104 | bytes 7500000 | tf_op jit(solution)/shard_map/to_longitudes/pallas_call | solution.py:179
  154.6 5.7 %all-to-all-start.4 = ((bf16[8,2,4,96,256]{4,3,2,1,0:T(8,128)(2,1)}), bf16[8,2,4,96,256]{4,3,2,1,0:T(8,128)(2,1)}, u32[]{:S(2)}, u32[]{:S(2)}) async-start(bf16[8,2,4,96,256]{4,3,2,1,0:T(8,128)(2,1)} %to_longitudes.5), calls=%async_computation.4 | async-start | bytes 6291456 | tf_op jit(solution)/shard_map/all_to_all | solution.py:242
  160.3 5.6 %to_modes.4.m_ref = bf16[16,64,768]{2,1,0:T(8,128)(2,1)} custom-call(bf16[768,768]{1,0:T(8,128)(2,1)} %copy.26.t_ref, bf16[256,256]{1,0:T(8,128)(2,1)} %fusion.7.p_ref, bf16[8,4,96,256]{3,2,1,0:T(8,128)(2,1)} %all_to_all.45.x_ref), custom_call_target="tpu_custom_call" | custom-call | flops 1207959552 | bytes 4500000 | tf_op jit(solution)/shard_map/to_modes/pallas_call | solution.py:99
  165.9 1.9 collective-permute-start.1
  167.8 2.6 collective-permute-start
  170.4 25.0 %collective-permute-done.1.r_ref = bf16[16,64,768]{2,1,0:T(8,128)(2,1)} collective-permute-done((bf16[16,64,768]{2,1,0:T(8,128)(2,1)}, bf16[16,64,768]{2,1,0:T(8,128)(2,1)}, u32[]{:S(2)}, u32[]{:S(2)}) %collective-permute-start.1) | collective-permute-done | bytes 1572896 | tf_op jit(solution)/shard_map/ppermute | solution.py:249
  195.4 20.2 %collective-permute-done.l_ref = bf16[16,64,768]{2,1,0:T(8,128)(2,1)} collective-permute-done((bf16[16,64,768]{2,1,0:T(8,128)(2,1)}, bf16[16,64,768]{2,1,0:T(8,128)(2,1)}, u32[]{:S(2)}, u32[]{:S(2)}) %collective-permute-start) | collective-permute-done | bytes 1572896 | tf_op jit(solution)/shard_map/ppermute | solution.py:248
  215.6 6.3 %couple.4.b_ref = bf16[2,16,64,768]{3,2,1,0:T(8,128)(2,1)} custom-call(bf16[3,128,64]{2,1,0:T(8,128)(2,1)} %pad_maximum_fusion.1.a_ref, f32[12,384]{1,0:T(8,128)} %slice.13.f_ref, bf16[16,64,768]{2,1,0:T(8,128)(2,1)} %collective-permute-done.l_ref, bf16[16,64,768]{2,1,0:T(8,128)(2,1)} %to_modes.4.m_ref, bf16[16,64,768]{2,1,0:T(8,128)(2,1)} %collective-permute-done.1.r_ref), custom_call_target="tpu_custom_call" | custom-call | flops 2415919104 | bytes 8000000 | tf_op jit(solution)/shard_map/couple/pallas_call | solution.py:148
  221.9 9.4 %to_longitudes.4 = bf16[8,2,4,96,256]{4,3,2,1,0:T(8,128)(2,1)} custom-call(bf16[768,768]{1,0:T(8,128)(2,1)} %bitcast.114, bf16[256,256]{1,0:T(8,128)(2,1)} %fusion.7.p_ref, bf16[2,16,64,768]{3,2,1,0:T(8,128)(2,1)} %couple.4.b_ref), custom_call_target="tpu_custom_call" | custom-call | flops 2415919104 | bytes 7500000 | tf_op jit(solution)/shard_map/to_longitudes/pallas_call | solution.py:179
  231.2 5.5 %all-to-all-start.2 = ((bf16[8,2,4,96,256]{4,3,2,1,0:T(8,128)(2,1)}), bf16[8,2,4,96,256]{4,3,2,1,0:T(8,128)(2,1)}, u32[]{:S(2)}, u32[]{:S(2)}) async-start(bf16[8,2,4,96,256]{4,3,2,1,0:T(8,128)(2,1)} %to_longitudes.4), calls=%async_computation.2 | async-start | bytes 6291456 | tf_op jit(solution)/shard_map/all_to_all | solution.py:242
  236.8 1.5 copy.35.t_ref
  238.3 5.7 %to_modes.7.m_ref = bf16[16,64,768]{2,1,0:T(8,128)(2,1)} custom-call(bf16[768,768]{1,0:T(8,128)(2,1)} %copy.35.t_ref, bf16[256,256]{1,0:T(8,128)(2,1)} %fusion.7.p_ref, bf16[8,4,96,256]{3,2,1,0:T(8,128)(2,1)} %all-to-all-done.7.x_ref), custom_call_target="tpu_custom_call" | custom-call | flops 1207959552 | bytes 4500000 | tf_op jit(solution)/shard_map/to_modes/pallas_call | solution.py:99
  244.0 1.9 collective-permute-start.7
  245.9 2.4 collective-permute-start.6
  251.5 21.1 %collective-permute-done.7.r_ref = bf16[16,64,768]{2,1,0:T(8,128)(2,1)} collective-permute-done((bf16[16,64,768]{2,1,0:T(8,128)(2,1)}, bf16[16,64,768]{2,1,0:T(8,128)(2,1)}, u32[]{:S(2)}, u32[]{:S(2)}) %collective-permute-start.7) | collective-permute-done | bytes 1572896 | tf_op jit(solution)/shard_map/ppermute | solution.py:249
  272.5 6.3 %couple.7.b_ref = bf16[2,16,64,768]{3,2,1,0:T(8,128)(2,1)} custom-call(bf16[3,128,64]{2,1,0:T(8,128)(2,1)} %pad_maximum_fusion.2.a_ref, f32[12,384]{1,0:T(8,128)} %slice.15.f_ref, bf16[16,64,768]{2,1,0:T(8,128)(2,1)} %collective-permute-done.6.l_ref, bf16[16,64,768]{2,1,0:T(8,128)(2,1)} %to_modes.7.m_ref, bf16[16,64,768]{2,1,0:T(8,128)(2,1)} %collective-permute-done.7.r_ref), custom_call_target="tpu_custom_call" | custom-call | flops 2415919104 | bytes 8000000 | tf_op jit(solution)/shard_map/couple/pallas_call | solution.py:148
  278.8 9.4 %to_longitudes.7 = bf16[8,2,4,96,256]{4,3,2,1,0:T(8,128)(2,1)} custom-call(bf16[768,768]{1,0:T(8,128)(2,1)} %fusion.40.t_ref, bf16[256,256]{1,0:T(8,128)(2,1)} %fusion.7.p_ref, bf16[2,16,64,768]{3,2,1,0:T(8,128)(2,1)} %couple.7.b_ref), custom_call_target="tpu_custom_call" | custom-call | flops 2415919104 | bytes 7500000 | tf_op jit(solution)/shard_map/to_longitudes/pallas_call | solution.py:179
  288.2 5.4 %all-to-all-start.8 = ((bf16[8,2,4,96,256]{4,3,2,1,0:T(8,128)(2,1)}), bf16[8,2,4,96,256]{4,3,2,1,0:T(8,128)(2,1)S(1)}, u32[]{:S(2)}, u32[]{:S(2)}) async-start(bf16[8,2,4,96,256]{4,3,2,1,0:T(8,128)(2,1)} %to_longitudes.7), calls=%async_computation.8 | async-start | bytes 6291456 | tf_op jit(solution)/shard_map/all_to_all | solution.py:242
  293.6 5.6 %to_modes.6.m_ref = bf16[16,64,768]{2,1,0:T(8,128)(2,1)} custom-call(bf16[768,768]{1,0:T(8,128)(2,1)} %copy.35.t_ref, bf16[256,256]{1,0:T(8,128)(2,1)} %fusion.7.p_ref, bf16[8,4,96,256]{3,2,1,0:T(8,128)(2,1)} %all-to-all-done.5.x_ref), custom_call_target="tpu_custom_call" | custom-call | flops 1207959552 | bytes 4500000 | tf_op jit(solution)/shard_map/to_modes/pallas_call | solution.py:99
  299.2 6.9 %collective-permute-start.5 = (bf16[16,64,768]{2,1,0:T(8,128)(2,1)}, bf16[16,64,768]{2,1,0:T(8,128)(2,1)}, u32[]{:S(2)}, u32[]{:S(2)}) collective-permute-start(bf16[16,64,768]{2,1,0:T(8,128)(2,1)} %to_modes.6.m_ref), channel_id=1, source_target_pairs={{8,0},{16,8},{24,16},{32,24},{40,32},{48,40},{56,48},{64,56},{72,6... | collective-permute-start | bytes 4718600 | tf_op jit(solution)/shard_map/ppermute | solution.py:249
  306.1 1.9 collective-permute-start.4
  308.0 30.0 %collective-permute-done.5.r_ref = bf16[16,64,768]{2,1,0:T(8,128)(2,1)} collective-permute-done((bf16[16,64,768]{2,1,0:T(8,128)(2,1)}, bf16[16,64,768]{2,1,0:T(8,128)(2,1)}, u32[]{:S(2)}, u32[]{:S(2)}) %collective-permute-start.5) | collective-permute-done | bytes 1572896 | tf_op jit(solution)/shard_map/ppermute | solution.py:249
  338.1 6.3 %couple.6.b_ref = bf16[2,16,64,768]{3,2,1,0:T(8,128)(2,1)} custom-call(bf16[3,128,64]{2,1,0:T(8,128)(2,1)} %pad_maximum_fusion.2.a_ref, f32[12,384]{1,0:T(8,128)} %slice.15.f_ref, bf16[16,64,768]{2,1,0:T(8,128)(2,1)} %collective-permute-done.4.l_ref, bf16[16,64,768]{2,1,0:T(8,128)(2,1)} %to_modes.6.m_ref, bf16[16,64,768]{2,1,0:T(8,128)(2,1)} %collective-permute-done.5.r_ref), custom_call_target="tpu_custom_call" | custom-call | flops 2415919104 | bytes 8000000 | tf_op jit(solution)/shard_map/couple/pallas_call | solution.py:148
  344.4 9.4 %to_longitudes.6 = bf16[8,2,4,96,256]{4,3,2,1,0:T(8,128)(2,1)} custom-call(bf16[768,768]{1,0:T(8,128)(2,1)} %fusion.40.t_ref, bf16[256,256]{1,0:T(8,128)(2,1)} %fusion.7.p_ref, bf16[2,16,64,768]{3,2,1,0:T(8,128)(2,1)} %couple.6.b_ref), custom_call_target="tpu_custom_call" | custom-call | flops 2415919104 | bytes 7500000 | tf_op jit(solution)/shard_map/to_longitudes/pallas_call | solution.py:179
  353.7 1.7 copy-done
  355.4 6.5 %all-to-all-start.6 = ((bf16[8,2,4,96,256]{4,3,2,1,0:T(8,128)(2,1)}), bf16[8,2,4,96,256]{4,3,2,1,0:T(8,128)(2,1)}, u32[]{:S(2)}, u32[]{:S(2)}) async-start(bf16[8,2,4,96,256]{4,3,2,1,0:T(8,128)(2,1)} %to_longitudes.6), calls=%async_computation.6 | async-start | bytes 6291456 | tf_op jit(solution)/shard_map/all_to_all | solution.py:242
  361.8 15.7 %mix.2 = bf16[64,96,256]{2,1,0:T(8,128)(2,1)} custom-call(bf16[2,256,256]{2,1,0:T(8,128)(2,1)} %refs_0_.3, bf16[8,2,4,96,256]{4,3,2,1,0:T(8,128)(2,1)} %all-to-all-done.2.refs_1_, bf16[8,2,4,96,256]{4,3,2,1,0:T(8,128)(2,1)} %all-to-all-done.4.refs_2_), custom_call_target="tpu_custom_call" | custom-call | flops 1610612736 | bytes 9500000 | tf_op jit(solution)/shard_map/mix/pallas_call | solution.py:224
  377.5 9.9 %all-to-all-done.6.refs_1_ = bf16[8,2,4,96,256]{4,3,2,1,0:T(8,128)(2,1)} async-done(((bf16[8,2,4,96,256]{4,3,2,1,0:T(8,128)(2,1)}), bf16[8,2,4,96,256]{4,3,2,1,0:T(8,128)(2,1)}, u32[]{:S(2)}, u32[]{:S(2)}) %all-to-all-start.6) | async-done | bytes 3145760 | tf_op jit(solution)/shard_map/all_to_all | solution.py:242
  387.4 15.7 %mix.3 = bf16[64,96,256]{2,1,0:T(8,128)(2,1)} custom-call(bf16[2,256,256]{2,1,0:T(8,128)(2,1)} %refs_0_.3, bf16[8,2,4,96,256]{4,3,2,1,0:T(8,128)(2,1)} %all-to-all-done.6.refs_1_, bf16[8,2,4,96,256]{4,3,2,1,0:T(8,128)(2,1)} %copy-done), custom_call_target="tpu_custom_call" | custom-call | flops 1610612736 | bytes 9500000 | tf_op jit(solution)/shard_map/mix/pallas_call | solution.py:224
  (116 shorter events, 13.5 us)
Async XLA Ops:
  3.9 2.5 copy-start.20
  4.0 2.5 copy-start.22
  4.0 2.5 copy-start.24
  4.0 2.5 copy-start.26
  4.0 2.5 copy-start.28
  4.0 2.5 copy-start.30
  4.7 1.6 copy-start.12
  4.7 1.6 copy-start.14
  5.4 1.1 copy-start.16
  5.4 1.1 copy-start.18
  8.0 16.4 %all-to-all-start = ((f32[8,9,128]{2,1,0:T(8,128)}), f32[8,9,128]{2,1,0:T(8,128)S(1)}, u32[]{:S(2)}, u32[]{:S(2)}) async-start(f32[8,9,128]{2,1,0:T(8,128)} %broadcast_in_dim.194), calls=%async_computation | async-start | bytes 131072 | tf_op jit(solution)/shard_map/all_to_all | solution.py:242
  24.4 23.9 %copy-start.3 = (f32[8,9,128]{2,1,0:T(8,128)}, f32[8,9,128]{2,1,0:T(8,128)S(1)}, u32[]{:S(2)}) copy-start(f32[8,9,128]{2,1,0:T(8,128)S(1)} %all-to-all-done) | copy-start | bytes 110596
  48.3 23.7 %all-to-all-start.3 = ((bf16[8,4,96,256]{3,2,1,0:T(8,128)(2,1)}), bf16[8,4,96,256]{3,2,1,0:T(8,128)(2,1)S(1)}, u32[]{:S(2)}, u32[]{:S(2)}) async-start(bf16[8,4,96,256]{3,2,1,0:T(8,128)(2,1)} %get-tuple-element.7), calls=%async_computation.3 | async-start | bytes 3145728 | tf_op jit(solution)/shard_map/all_to_all | solution.py:242
  72.0 1.1 copy-start.2
  73.1 29.4 %all-to-all-start.5 = ((bf16[8,4,96,256]{3,2,1,0:T(8,128)(2,1)}), bf16[8,4,96,256]{3,2,1,0:T(8,128)(2,1)}, u32[]{:S(2)}, u32[]{:S(2)}) async-start(bf16[8,4,96,256]{3,2,1,0:T(8,128)(2,1)} %get-tuple-element.8), calls=%async_computation.5 | async-start | bytes 3145728 | tf_op jit(solution)/shard_map/all_to_all | solution.py:242
  87.2 13.3 %copy-start.13 = (pred[6]{0:T(512)(128)(4,1)S(1)}, pred[6]{0:T(512)(128)(4,1)}, u32[]{:S(2)}) copy-start(pred[6]{0:T(512)(128)(4,1)} %copy-done.12) | copy-start | bytes 22
  87.2 13.3 %copy-start.15 = (pred[6]{0:T(512)(128)(4,1)S(1)}, pred[6]{0:T(512)(128)(4,1)}, u32[]{:S(2)}) copy-start(pred[6]{0:T(512)(128)(4,1)} %copy-done.14) | copy-start | bytes 22
  87.2 13.3 %copy-start.17 = (pred[6]{0:T(512)(128)(4,1)S(1)}, pred[6]{0:T(512)(128)(4,1)}, u32[]{:S(2)}) copy-start(pred[6]{0:T(512)(128)(4,1)} %copy-done.16) | copy-start | bytes 22
  87.2 13.3 %copy-start.19 = (pred[6]{0:T(512)(128)(4,1)S(1)}, pred[6]{0:T(512)(128)(4,1)}, u32[]{:S(2)}) copy-start(pred[6]{0:T(512)(128)(4,1)} %copy-done.18) | copy-start | bytes 22
  87.2 13.3 %copy-start.21 = (pred[6]{0:T(512)(128)(4,1)S(1)}, pred[6]{0:T(512)(128)(4,1)}, u32[]{:S(2)}) copy-start(pred[6]{0:T(512)(128)(4,1)} %copy-done.20) | copy-start | bytes 22
  87.2 13.3 %copy-start.23 = (pred[6]{0:T(512)(128)(4,1)S(1)}, pred[6]{0:T(512)(128)(4,1)}, u32[]{:S(2)}) copy-start(pred[6]{0:T(512)(128)(4,1)} %copy-done.22) | copy-start | bytes 22
  87.2 13.3 %copy-start.25 = (pred[6]{0:T(512)(128)(4,1)S(1)}, pred[6]{0:T(512)(128)(4,1)}, u32[]{:S(2)}) copy-start(pred[6]{0:T(512)(128)(4,1)} %copy-done.24) | copy-start | bytes 22
  87.2 13.3 %copy-start.27 = (pred[6]{0:T(512)(128)(4,1)S(1)}, pred[6]{0:T(512)(128)(4,1)}, u32[]{:S(2)}) copy-start(pred[6]{0:T(512)(128)(4,1)} %copy-done.26) | copy-start | bytes 22
  87.2 13.3 %copy-start.29 = (pred[6]{0:T(512)(128)(4,1)S(1)}, pred[6]{0:T(512)(128)(4,1)}, u32[]{:S(2)}) copy-start(pred[6]{0:T(512)(128)(4,1)} %copy-done.28) | copy-start | bytes 22
  87.2 13.3 %copy-start.31 = (pred[6]{0:T(512)(128)(4,1)S(1)}, pred[6]{0:T(512)(128)(4,1)}, u32[]{:S(2)}) copy-start(pred[6]{0:T(512)(128)(4,1)} %copy-done.30) | copy-start | bytes 22
  92.9 38.6 %collective-permute-start.3 = (bf16[16,64,768]{2,1,0:T(8,128)(2,1)}, bf16[16,64,768]{2,1,0:T(8,128)(2,1)}, u32[]{:S(2)}, u32[]{:S(2)}) collective-permute-start(bf16[16,64,768]{2,1,0:T(8,128)(2,1)} %to_modes.5.m_ref), channel_id=1, source_target_pairs={{8,0},{16,8},{24,16},{32,24},{40,32},{48,40},{56,48},{64,56},{72,6... | collective-permute-start | bytes 4718600 | tf_op jit(solution)/shard_map/ppermute | solution.py:249
  98.5 40.4 %collective-permute-start.2 = (bf16[16,64,768]{2,1,0:T(8,128)(2,1)}, bf16[16,64,768]{2,1,0:T(8,128)(2,1)}, u32[]{:S(2)}, u32[]{:S(2)}) collective-permute-start(bf16[16,64,768]{2,1,0:T(8,128)(2,1)} %to_modes.5.m_ref), channel_id=1, source_target_pairs={{0,8},{8,16},{16,24},{24,32},{32,40},{40,48},{48,56},{56,64},{64,7... | collective-permute-start | bytes 4718600 | tf_op jit(solution)/shard_map/ppermute | solution.py:248
  102.5 0.6 copy-start.6
  103.1 51.5 %all-to-all-start.7 = ((bf16[8,4,96,256]{3,2,1,0:T(8,128)(2,1)}), bf16[8,4,96,256]{3,2,1,0:T(8,128)(2,1)}, u32[]{:S(2)}, u32[]{:S(2)}) async-start(bf16[8,4,96,256]{3,2,1,0:T(8,128)(2,1)} %get-tuple-element.9), calls=%async_computation.7 | async-start | bytes 3145728 | tf_op jit(solution)/shard_map/all_to_all | solution.py:242
  109.5 1.2 copy-start.4
  154.6 76.6 %all-to-all-start.4 = ((bf16[8,2,4,96,256]{4,3,2,1,0:T(8,128)(2,1)}), bf16[8,2,4,96,256]{4,3,2,1,0:T(8,128)(2,1)}, u32[]{:S(2)}, u32[]{:S(2)}) async-start(bf16[8,2,4,96,256]{4,3,2,1,0:T(8,128)(2,1)} %to_longitudes.5), calls=%async_computation.4 | async-start | bytes 6291456 | tf_op jit(solution)/shard_map/all_to_all | solution.py:242
  165.9 29.5 %collective-permute-start.1 = (bf16[16,64,768]{2,1,0:T(8,128)(2,1)}, bf16[16,64,768]{2,1,0:T(8,128)(2,1)}, u32[]{:S(2)}, u32[]{:S(2)}) collective-permute-start(bf16[16,64,768]{2,1,0:T(8,128)(2,1)} %to_modes.4.m_ref), channel_id=1, source_target_pairs={{8,0},{16,8},{24,16},{32,24},{40,32},{48,40},{56,48},{64,56},{72,6... | collective-permute-start | bytes 4718600 | tf_op jit(solution)/shard_map/ppermute | solution.py:249
  167.8 47.8 %collective-permute-start = (bf16[16,64,768]{2,1,0:T(8,128)(2,1)}, bf16[16,64,768]{2,1,0:T(8,128)(2,1)}, u32[]{:S(2)}, u32[]{:S(2)}) collective-permute-start(bf16[16,64,768]{2,1,0:T(8,128)(2,1)} %to_modes.4.m_ref), channel_id=1, source_target_pairs={{0,8},{8,16},{16,24},{24,32},{32,40},{40,48},{48,56},{56,64},{64,7... | collective-permute-start | bytes 4718600 | tf_op jit(solution)/shard_map/ppermute | solution.py:248
  231.2 5.6 %copy-start.1 = (bf16[768,768]{0,1:T(8,128)(2,1)S(1)}, bf16[768,768]{0,1:T(8,128)(2,1)}, u32[]{:S(2)}) copy-start(bf16[768,768]{0,1:T(8,128)(2,1)} %multiply_convert_fusion) | copy-start | bytes 3538948
  231.2 57.0 %all-to-all-start.2 = ((bf16[8,2,4,96,256]{4,3,2,1,0:T(8,128)(2,1)}), bf16[8,2,4,96,256]{4,3,2,1,0:T(8,128)(2,1)}, u32[]{:S(2)}, u32[]{:S(2)}) async-start(bf16[8,2,4,96,256]{4,3,2,1,0:T(8,128)(2,1)} %to_longitudes.4), calls=%async_computation.2 | async-start | bytes 6291456 | tf_op jit(solution)/shard_map/all_to_all | solution.py:242
  238.3 10.0 %copy-start.7 = (bf16[64,64]{1,0:T(8,128)(2,1)S(1)}, bf16[64,64]{1,0:T(8,128)(2,1)}, u32[]{:S(2)}) copy-start(bf16[64,64]{1,0:T(8,128)(2,1)} %copy-done.6) | copy-start | bytes 24580
  238.3 10.2 %copy-start.11 = (bf16[64,64]{1,0:T(8,128)(2,1)S(1)}, bf16[64,64]{1,0:T(8,128)(2,1)}, u32[]{:S(2)}) copy-start(bf16[64,64]{1,0:T(8,128)(2,1)} %get-tuple-element.10) | copy-start | bytes 24580
  238.3 10.3 %copy-start.10 = (bf16[64,64]{1,0:T(8,128)(2,1)S(1)}, bf16[64,64]{1,0:T(8,128)(2,1)}, u32[]{:S(2)}) copy-start(bf16[64,64]{1,0:T(8,128)(2,1)} %get-tuple-element.16) | copy-start | bytes 24580
  238.3 10.4 %copy-start.9 = (bf16[64,64]{1,0:T(8,128)(2,1)S(1)}, bf16[64,64]{1,0:T(8,128)(2,1)}, u32[]{:S(2)}) copy-start(bf16[64,64]{1,0:T(8,128)(2,1)} %get-tuple-element.17) | copy-start | bytes 24580
  238.3 10.5 %copy-start.8 = (bf16[64,64]{1,0:T(8,128)(2,1)S(1)}, bf16[64,64]{1,0:T(8,128)(2,1)}, u32[]{:S(2)}) copy-start(bf16[64,64]{1,0:T(8,128)(2,1)} %get-tuple-element.19) | copy-start | bytes 24580
  244.0 28.6 %collective-permute-start.7 = (bf16[16,64,768]{2,1,0:T(8,128)(2,1)}, bf16[16,64,768]{2,1,0:T(8,128)(2,1)}, u32[]{:S(2)}, u32[]{:S(2)}) collective-permute-start(bf16[16,64,768]{2,1,0:T(8,128)(2,1)} %to_modes.7.m_ref), channel_id=1, source_target_pairs={{8,0},{16,8},{24,16},{32,24},{40,32},{48,40},{56,48},{64,56},{72,6... | collective-permute-start | bytes 4718600 | tf_op jit(solution)/shard_map/ppermute | solution.py:249
  245.9 26.7 %collective-permute-start.6 = (bf16[16,64,768]{2,1,0:T(8,128)(2,1)}, bf16[16,64,768]{2,1,0:T(8,128)(2,1)}, u32[]{:S(2)}, u32[]{:S(2)}) collective-permute-start(bf16[16,64,768]{2,1,0:T(8,128)(2,1)} %to_modes.7.m_ref), channel_id=1, source_target_pairs={{0,8},{8,16},{16,24},{24,32},{32,40},{40,48},{48,56},{56,64},{64,7... | collective-permute-start | bytes 4718600 | tf_op jit(solution)/shard_map/ppermute | solution.py:248
  249.6 1.1 copy-start.5
  288.2 65.5 %all-to-all-start.8 = ((bf16[8,2,4,96,256]{4,3,2,1,0:T(8,128)(2,1)}), bf16[8,2,4,96,256]{4,3,2,1,0:T(8,128)(2,1)S(1)}, u32[]{:S(2)}, u32[]{:S(2)}) async-start(bf16[8,2,4,96,256]{4,3,2,1,0:T(8,128)(2,1)} %to_longitudes.7), calls=%async_computation.8 | async-start | bytes 6291456 | tf_op jit(solution)/shard_map/all_to_all | solution.py:242
  299.2 38.8 %collective-permute-start.5 = (bf16[16,64,768]{2,1,0:T(8,128)(2,1)}, bf16[16,64,768]{2,1,0:T(8,128)(2,1)}, u32[]{:S(2)}, u32[]{:S(2)}) collective-permute-start(bf16[16,64,768]{2,1,0:T(8,128)(2,1)} %to_modes.6.m_ref), channel_id=1, source_target_pairs={{8,0},{16,8},{24,16},{32,24},{40,32},{48,40},{56,48},{64,56},{72,6... | collective-permute-start | bytes 4718600 | tf_op jit(solution)/shard_map/ppermute | solution.py:249
  306.1 32.0 %collective-permute-start.4 = (bf16[16,64,768]{2,1,0:T(8,128)(2,1)}, bf16[16,64,768]{2,1,0:T(8,128)(2,1)}, u32[]{:S(2)}, u32[]{:S(2)}) collective-permute-start(bf16[16,64,768]{2,1,0:T(8,128)(2,1)} %to_modes.6.m_ref), channel_id=1, source_target_pairs={{0,8},{8,16},{16,24},{24,32},{32,40},{40,48},{48,56},{56,64},{64,7... | collective-permute-start | bytes 4718600 | tf_op jit(solution)/shard_map/ppermute | solution.py:248
  353.7 1.7 copy-start
  355.4 32.0 %all-to-all-start.6 = ((bf16[8,2,4,96,256]{4,3,2,1,0:T(8,128)(2,1)}), bf16[8,2,4,96,256]{4,3,2,1,0:T(8,128)(2,1)}, u32[]{:S(2)}, u32[]{:S(2)}) async-start(bf16[8,2,4,96,256]{4,3,2,1,0:T(8,128)(2,1)} %to_longitudes.6), calls=%async_computation.6 | async-start | bytes 6291456 | tf_op jit(solution)/shard_map/all_to_all | solution.py:242
